TPU v7x, 128 devices: a whole 4x4x4 slice. The times are simulated.
128 devices in a mesh: section: 4 (over x), vertex: 16 (over z, y), feat: 2 (over core).
Axes of the slice: x: 4, y: 4, z: 4, core: 2. Of those that a mesh axis runs over, the one named last changes fastest.
Arguments:
- features: bfloat16 [32768, 1024], P('vertex', 'feat'), may hold values from -6 to 6
- history: bfloat16 [4, 32768, 1024], P('section', 'vertex', 'feat'), may hold values from -6 to 6
- weights: bfloat16 [4, 1024, 1024], P('section', None, 'feat'), may hold values from -0.1875 to 0.1875
- tile_values: bfloat16 [3, 1024, 128, 128], P(None, 'vertex'), may hold values from -0.125 to 0.125
- tile_rows: int32 [3, 1024], P(None, 'vertex'), may hold values from 0 to 15, as said below
- tile_cols: int32 [3, 1024], P(None, 'vertex'), may hold values from 0 to 15
- tile_counts: int32 [3, 16], P(None, 'vertex'), may hold values from 1 to 64, as said below
- span_ids: int32 [3, 2048], P(None, 'vertex'), may hold values from 0 to 2047, as said below
Outputs:
- layer_out: bfloat16 [4, 3, 2048, 1024], P('section', None, 'vertex', 'feat')
- new_history: bfloat16 [4, 32768, 1024], P('section', 'vertex', 'feat')
Inputs may be any that keep to these rules, and one draw needn't show every extreme that they name: `tile_rows`: within one owner's list for one block the (row block, column block) pairs are distinct. `tile_counts`: in every block some owner has exactly 64 live tiles. `span_ids`: the 384 entries of one owner over all blocks are distinct.
All inputs are finite; a program needn't handle non-finite values.
Results may differ from a plain program's by a relative error of at most 0.018.
Values may be sent and summed in bfloat16 or wider, within the bound.
No kernel may reach another device: no remote copies, remote signals or barrier semaphores. Data moves between devices by JAX's collectives and lax.ppermute only.
A program may use at most 128 MiB of HBM per device.

v0:
```python
import math

import jax
import jax.numpy as jnp
from jax import lax
from jax.experimental import pallas as pl
from jax.experimental.pallas import tpu as pltpu
from jax.sharding import PartitionSpec as P

RESIDUAL_SHARE = 0.2
BETA_SCALE = 0.5
MIB = 1 << 20


def rotated(array, axis, by):
    devices = lax.axis_size(axis)
    return lax.ppermute(array, axis, [(i, (i + by) % devices) for i in range(devices)])


def vmem_params(mib):
    return pltpu.CompilerParams(vmem_limit_bytes=mib * MIB)


def dense_adjacency(tile_values, tile_rows, tile_cols, tile_counts, row_blocks, col_blocks):
    spans, slots, side, _ = tile_values.shape
    rows, cols = row_blocks * side, col_blocks * side

    def kernel(rows_ref, cols_ref, counts_ref, values_ref, out_ref):
        span = pl.program_id(0)
        out_ref[...] = jnp.zeros_like(out_ref)

        @pl.loop(0, counts_ref[span])
        def _(slot):
            row = pl.multiple_of(rows_ref[span, slot] * side, side)
            col = pl.multiple_of(cols_ref[span, slot] * side, side)
            out_ref[0, pl.ds(row, side), pl.ds(col, side)] = values_ref[0, slot]

    return pl.pallas_call(
        kernel,
        out_shape=jax.ShapeDtypeStruct((spans, rows, cols), jnp.bfloat16),
        grid_spec=pltpu.PrefetchScalarGridSpec(
            num_scalar_prefetch=3,
            grid=(spans,),
            in_specs=[pl.BlockSpec((1, slots, side, side), lambda c, *_: (c, 0, 0, 0))],
            out_specs=pl.BlockSpec((1, rows, cols), lambda c, *_: (c, 0, 0)),
        ),
        compiler_params=vmem_params(40),
        cost_estimate=pl.CostEstimate(
            flops=0, transcendentals=0, bytes_accessed=2 * spans * (rows * cols + slots * side * side)
        ),
        name="dense_adjacency",
    )(tile_rows, tile_cols, tile_counts[:, 0], tile_values)


def first_partial(adjacency, hist, feats, replaced, row_devices):
    spans, rows, cols = adjacency.shape
    width = hist.shape[1]
    rows_local = rows // row_devices
    step = 2

    def kernel(adj_ref, hist_ref, feat_ref, mask_ref, out_ref, table):
        table[...] = jnp.where(mask_ref[0] > 0, feat_ref[...], hist_ref[...])
        for first in range(0, row_devices, step):
            part = jnp.dot(
                adj_ref[0, first * rows_local : (first + step) * rows_local, :],
                table[...],
                preferred_element_type=jnp.float32,
            )
            out_ref[first : first + step, 0] = part.astype(jnp.bfloat16).reshape(
                step, rows_local, width
            )

    return pl.pallas_call(
        kernel,
        out_shape=jax.ShapeDtypeStruct((row_devices, spans, rows_local, width), jnp.bfloat16),
        grid=(spans,),
        in_specs=[
            pl.BlockSpec((1, rows, cols), lambda c: (c, 0, 0)),
            pl.BlockSpec((cols, width), lambda c: (0, 0)),
            pl.BlockSpec((cols, width), lambda c: (0, 0)),
            pl.BlockSpec((1, cols, width), lambda c: (c, 0, 0)),
        ],
        out_specs=pl.BlockSpec((row_devices, 1, rows_local, width), lambda c: (0, c, 0, 0)),
        scratch_shapes=[pltpu.VMEM((cols, width), jnp.bfloat16)],
        compiler_params=vmem_params(40),
        cost_estimate=pl.CostEstimate(
            flops=2 * spans * rows * cols * width,
            transcendentals=0,
            bytes_accessed=2 * spans * (rows * cols + rows * width),
        ),
        name="first_partial",
    )(adjacency, hist, feats, replaced)


def static_parts(adjacency, hist_slices, replaced, select):
    spans, rows, cols = adjacency.shape
    layers, _, width = hist_slices.shape
    later = layers - 1
    picks = select.shape[1]
    chunk = 256

    def kernel(adj_ref, hist_ref, mask_ref, sel_ref, static_ref, cols_ref, right):
        for layer in range(later):
            right[:, layer * width : (layer + 1) * width] = jnp.where(
                mask_ref[0] > 0, jnp.zeros_like(hist_ref[0]), hist_ref[layer + 1]
            )
        right[:, later * width :] = sel_ref[...]
        for first in range(0, rows, chunk):
            part = jnp.dot(
                adj_ref[0, first : first + chunk, :], right[...], preferred_element_type=jnp.float32
            )
            for layer in range(later):
                static_ref[layer, 0, first : first + chunk] = part[
                    :, layer * width : (layer + 1) * width
                ]
            cols_ref[0, first : first + chunk] = part[:, later * width :].astype(jnp.bfloat16)

    return pl.pallas_call(
        kernel,
        out_shape=(
            jax.ShapeDtypeStruct((later, spans, rows, width), jnp.float32),
            jax.ShapeDtypeStruct((spans, rows, picks), jnp.bfloat16),
        ),
        grid=(spans,),
        in_specs=[
            pl.BlockSpec((1, rows, cols), lambda c: (c, 0, 0)),
            pl.BlockSpec((layers, cols, width), lambda c: (0, 0, 0)),
            pl.BlockSpec((1, cols, width), lambda c: (c, 0, 0)),
            pl.BlockSpec((cols, picks), lambda c: (0, 0)),
        ],
        out_specs=(
            pl.BlockSpec((later, 1, rows, width), lambda c: (0, c, 0, 0)),
            pl.BlockSpec((1, rows, picks), lambda c: (c, 0, 0)),
        ),
        scratch_shapes=[pltpu.VMEM((cols, later * width + picks), jnp.bfloat16)],
        compiler_params=vmem_params(48),
        cost_estimate=pl.CostEstimate(
            flops=2 * spans * rows * cols * (later * width + picks),
            transcendentals=0,
            bytes_accessed=spans * (2 * rows * cols + 4 * later * rows * width + 2 * rows * picks),
        ),
        name="static_parts",
    )(adjacency, hist_slices, replaced, select)


def layer_step(gathered, support, weight_rows, static, columns, beta, row_devices):
    halves, parts, picks, width = gathered.shape
    spans, rows, _ = columns.shape
    rows_local = rows // row_devices
    depth = halves * parts * width
    step = 4

    def kernel(gath_ref, sup_ref, w_ref, static_ref, cols_ref, out_ref, left):
        for half in range(halves):
            for part in range(parts):
                first = (half * parts + part) * width
                left[:, first : first + width] = gath_ref[half, part]
        projected = jnp.dot(left[...], w_ref[...], preferred_element_type=jnp.float32)
        fresh = jnp.maximum(
            (1.0 - beta) * sup_ref[...].astype(jnp.float32) + beta * projected, 0.0
        ).astype(jnp.bfloat16)
        for span in range(spans):
            used = (span + 1) * rows_local
            for first in range(0, row_devices, step):
                at = slice(first * rows_local, (first + step) * rows_local)
                part = static_ref[span, at] + jnp.dot(
                    cols_ref[span, at, :used], fresh[:used], preferred_element_type=jnp.float32
                )
                out_ref[first : first + step, span] = part.astype(jnp.bfloat16).reshape(
                    step, rows_local, width
                )

    return pl.pallas_call(
        kernel,
        out_shape=jax.ShapeDtypeStruct((row_devices, spans, rows_local, width), jnp.bfloat16),
        scratch_shapes=[pltpu.VMEM((picks, depth), jnp.bfloat16)],
        compiler_params=vmem_params(40),
        cost_estimate=pl.CostEstimate(
            flops=2 * picks * depth * width + 4 * rows * width * picks,
            transcendentals=0,
            bytes_accessed=6 * spans * rows * width + 2 * spans * rows * picks,
        ),
        name="layer_step",
    )(gathered, support, weight_rows, static, columns)


def whole_rows(gathered, own_half, weight_cols, beta):
    halves, parts, picks, width = gathered.shape
    full = jnp.transpose(gathered, (2, 0, 1, 3)).reshape(picks, halves * parts * width)
    projected = jnp.dot(full, weight_cols, preferred_element_type=jnp.float32)
    return jax.nn.relu(
        (1.0 - beta) * own_half.astype(jnp.float32) + beta * projected
    ).astype(jnp.bfloat16)


def shards(features, history, weights, tile_values, tile_rows, tile_cols, tile_counts, span_ids):
    spans, rows_local = span_ids.shape
    side = tile_values.shape[2]
    owned, half = features.shape
    layers = lax.axis_size("section")
    halves = lax.axis_size("feat")
    row_devices = lax.axis_size("vertex")
    section = lax.axis_index("section")
    feat = lax.axis_index("feat")
    width = half // layers
    picks = spans * rows_local
    depth = weights.shape[1]
    betas = [math.log(BETA_SCALE / (layer + 1) + 1.0) for layer in range(layers)]

    def column_slices(array):
        return jnp.transpose(array.reshape(array.shape[0], layers, width), (1, 0, 2))

    stored = history[0]
    hist_slices = lax.all_to_all(column_slices(stored), "section", 0, 0, tiled=True)
    weight_slices = lax.all_to_all(column_slices(weights[0]), "section", 0, 0, tiled=True)
    weights_before = rotated(weights[0], "section", 1)

    ids = span_ids.reshape(picks)
    hits = jnp.arange(owned)[:, None] == ids[None, :]
    select = hits.astype(jnp.bfloat16)
    upto = jnp.stack([jnp.any(hits[:, : (c + 1) * rows_local], axis=1) for c in range(spans)])
    replaced = jnp.broadcast_to(upto[:, :, None], (spans, owned, width)).astype(jnp.bfloat16)

    feat_slice = lax.dynamic_slice_in_dim(features, section * width, width, 1)
    initial_half = jnp.take(features, ids, axis=0)
    initial = lax.dynamic_slice_in_dim(initial_half, section * width, width, 1).astype(jnp.float32)

    adjacency = dense_adjacency(
        tile_values, tile_rows, tile_cols, tile_counts, rows_local * row_devices // side, owned // side
    )
    partial = first_partial(adjacency, hist_slices[0], feat_slice, replaced, row_devices)
    statics, columns = static_parts(adjacency, hist_slices, replaced, select)

    order = (section - jnp.arange(layers)) % layers
    def in_order(weight):
        blocks = weight.reshape(halves, layers, width, weight.shape[-1])
        return jnp.take(blocks, order, axis=1).reshape(depth, weight.shape[-1])

    slices_ordered = [in_order(weight_slices[layer]) for layer in range(layers)]
    own_ordered = in_order(weights[0])
    before_ordered = in_order(weights_before)

    kept = kept_before = None
    for layer in range(layers):
        arrived = lax.all_to_all(partial, "vertex", 0, 0, tiled=True)
        aggregate = jnp.sum(arrived.astype(jnp.float32), axis=0).reshape(picks, width)
        support = (
            (1.0 - RESIDUAL_SHARE) * aggregate + RESIDUAL_SHARE * initial
        ).astype(jnp.bfloat16)
        near = jnp.stack([support] + [rotated(support, "section", by) for by in range(1, layers)])
        gathered = lax.all_gather(near, "feat", axis=0)
        if layer < layers - 1:
            partial = layer_step(
                gathered,
                support,
                slices_ordered[layer],
                statics[layer],
                columns,
                betas[layer],
                row_devices,
            )
        kept = gathered if kept is None else jnp.where(section == layer, gathered, kept)
        if layer < layers - 1:
            kept_before = (
                gathered
                if kept_before is None
                else jnp.where(section == layer + 1, gathered, kept_before)
            )

    def own_columns(array):
        mine = lax.dynamic_index_in_dim(array, feat, 0, keepdims=False)
        mine = jnp.take(mine, order, axis=0)
        return jnp.transpose(mine, (1, 0, 2)).reshape(picks, half)

    beta_rate = jnp.log(BETA_SCALE / (section + 1).astype(jnp.float32) + 1.0)
    beta_before = jnp.log(BETA_SCALE / jnp.maximum(section, 1).astype(jnp.float32) + 1.0)
    rows_before = whole_rows(kept_before, own_columns(kept_before), before_ordered, beta_before)
    fresh = jnp.where(section == 0, initial_half, rows_before)
    placed = jnp.dot(select, fresh, preferred_element_type=jnp.float32).astype(jnp.bfloat16)
    table = jnp.where(upto[spans - 1][:, None], placed, stored)
    rows_out = whole_rows(kept, own_columns(kept), own_ordered, beta_rate)
    return (rows_out.reshape(1, spans, rows_local, half), table[None])


def solution(mesh):
    placed = (
        P("vertex", "feat"),
        P("section", "vertex", "feat"),
        P("section", None, "feat"),
        P(None, "vertex", None, None),
        P(None, "vertex"),
        P(None, "vertex"),
        P(None, "vertex"),
        P(None, "vertex"),
    )
    return jax.shard_map(
        shards,
        mesh=mesh,
        in_specs=placed,
        out_specs=(P("section", None, "vertex", "feat"), P("section", "vertex", "feat")),
        check_vma=False,
    )
```

profile of v0, /device:TPU:1, one launch (start us, length us, event | category | flops | bytes accessed | tf_op | source)
XLA Modules:
  0.0 262.0 jit_solution(18359451715754422236)
XLA Ops:
  0.6 2.4 copy.45
  3.1 4.8 %all-to-all-start.2 = ((bf16[4,1024,128]{1,2,0:T(8,128)(2,1)}), bf16[4,1024,128]{1,2,0:T(8,128)(2,1)S(1)}, u32[]{:S(2)}, u32[]{:S(2)}) async-start(bf16[4,1024,128]{1,2,0:T(8,128)(2,1)} %bitcast.12), calls=%async_computation.2 | async-start | bytes 2097152 | tf_op jit(solution)/shard_map/all_to_all | solution.py:215
  7.9 3.9 %copy.43 = bf16[1,2048,512]{1,2,0:T(8,128)(2,1)} copy(bf16[1,2048,512]{2,1,0:T(8,128)(2,1)} %param.15) | data formatting | bytes 4194304 | tf_op args[1]
  11.8 4.0 %copy.44 = bf16[2048,4,128]{2,0,1:T(8,128)(2,1)} copy(bf16[2048,4,128]{0,2,1:T(8,128)(2,1)} %bitcast.149) | data formatting | bytes 4194304 | tf_op jit(solution)/shard_map/reshape;squeeze | solution.py:211
  15.9 1.9 fusion.2
  18.4 3.7 %all-to-all-done.2 = bf16[4,1024,128]{1,2,0:T(8,128)(2,1)S(1)} async-done(((bf16[4,1024,128]{1,2,0:T(8,128)(2,1)}), bf16[4,1024,128]{1,2,0:T(8,128)(2,1)S(1)}, u32[]{:S(2)}, u32[]{:S(2)}) %all-to-all-start.2) | async-done | bytes 1048608 | tf_op jit(solution)/shard_map/all_to_all | solution.py:215
  23.1 4.5 %all-to-all-start = ((bf16[4,2048,128]{2,1,0:T(8,128)(2,1)}), bf16[4,2048,128]{2,1,0:T(8,128)(2,1)}, u32[]{:S(2)}, u32[]{:S(2)}) async-start(bf16[4,2048,128]{2,1,0:T(8,128)(2,1)} %bitcast.148), calls=%async_computation | async-start | bytes 4194304 | tf_op jit(solution)/shard_map/all_to_all | solution.py:214
  27.7 2.1 gather_fusion
  29.8 2.8 %copy-done.3 = bf16[3,64,128,128]{3,2,1,0:T(8,128)(2,1)S(1)} copy-done((bf16[3,64,128,128]{3,2,1,0:T(8,128)(2,1)S(1)}, bf16[3,64,128,128]{3,2,1,0:T(8,128)(2,1)}, u32[]{:S(2)}) %copy-start.3) | copy-done | bytes 6291480
  32.6 9.8 %dense_adjacency.1.adj_ref = bf16[3,2048,2048]{2,1,0:T(8,128)(2,1)} custom-call(s32[3,64]{1,0:T(4,128)S(1)} %copy-done.5, s32[3,64]{1,0:T(4,128)S(1)} %copy-done.6, s32[3]{0:T(128)S(1)} %bitcast.147, bf16[3,64,128,128]{3,2,1,0:T(8,128)(2,1)S(1)} %copy-done.3), custom_call_target="tpu_custom_call" | custom-call | bytes 31457280 | tf_op jit(solution)/shard_map/dense_adjacency/pallas_call | solution.py:38
  46.9 5.2 %all-to-all-done.hist_ref = bf16[4,2048,128]{2,1,0:T(8,128)(2,1)} async-done(((bf16[4,2048,128]{2,1,0:T(8,128)(2,1)}), bf16[4,2048,128]{2,1,0:T(8,128)(2,1)}, u32[]{:S(2)}, u32[]{:S(2)}) %all-to-all-start) | async-done | bytes 2097184 | tf_op jit(solution)/shard_map/all_to_all | solution.py:214
  52.1 1.1 slice_bitcast_fusion.3.hist_ref
  54.2 12.9 %first_partial.1 = bf16[16,3,128,128]{3,2,1,0:T(8,128)(2,1)} custom-call(bf16[3,2048,2048]{2,1,0:T(8,128)(2,1)} %dense_adjacency.1.adj_ref, bf16[2048,128]{1,0:T(8,128)(2,1)S(1)} %slice_bitcast_fusion.3.hist_ref, bf16[2048,128]{1,0:T(8,128)(2,1)S(1)} %constant_dynamic-slice_fusion.feat_ref, bf16[3,2048,128]{2,1,0:T(8,128)(2,1)S(1)} %broadcast_in_dim.55.mask_ref), custom_call_target="tpu_custom_call" | custom-call | flops 3221225472 | bytes 26738688 | tf_op jit(solution)/shard_map/first_partial/pallas_call | solution.py:73
  67.1 7.8 %all-to-all-start.1 = ((bf16[16,3,128,128]{3,2,1,0:T(8,128)(2,1)}), bf16[16,3,128,128]{3,2,1,0:T(8,128)(2,1)}, u32[]{:S(2)}, u32[]{:S(2)}) async-start(bf16[16,3,128,128]{3,2,1,0:T(8,128)(2,1)} %first_partial.1), calls=%async_computation.1 | async-start | bytes 3145728 | tf_op jit(solution)/shard_map/all_to_all | solution.py:245
  74.9 1.4 copy-done.4
  76.3 26.7 %static_parts.1 = (f32[3,3,2048,128]{3,2,1,0:T(8,128)}, bf16[3,2048,384]{2,1,0:T(8,128)(2,1)}) custom-call(bf16[3,2048,2048]{2,1,0:T(8,128)(2,1)} %dense_adjacency.1.adj_ref, bf16[4,2048,128]{2,1,0:T(8,128)(2,1)} %all-to-all-done.hist_ref, bf16[3,2048,128]{2,1,0:T(8,128)(2,1)S(1)} %broadcast_in_dim.55.mask_ref, bf16[2048,384]{1,0:T(8,128)(2,1)S(1)} %copy-done.4), custom_call_target="tpu_custom_call" | custom-call | flops 19327352832 | bytes 39321600 | tf_op jit(solution)/shard_map/static_parts/pallas_call | solution.py:118
  103.1 1.7 convert_reduce_fusion.3
  105.2 1.8 collective-permute-start.1
  107.7 4.5 %slice_bitcast_fusion = (f32[3,2048,128]{2,1,0:T(8,128)S(1)}, f32[3,2048,128]{2,1,0:T(8,128)S(1)}, f32[3,2048,128]{2,1,0:T(8,128)S(1)}) fusion(f32[3,3,2048,128]{3,2,1,0:T(8,128)} %get-tuple-element.7), kind=kLoop, calls=%fused_computation.9 | loop fusion | bytes 18874368 | tf_op jit(solution)/shard_map/squeeze | solution.py:257
  112.3 5.6 %all-gather = bf16[8,384,128]{2,1,0:T(8,128)(2,1)S(1)} all-gather(bf16[4,384,128]{2,1,0:T(8,128)(2,1)S(1)} %pad_maximum_fusion), channel_id=2, replica_groups=mesh['section'=4,'vertex'=16,'feat'=2] {'feat'}, dimensions={0}, use_global_device_ids=true | all-gather | bytes 1179648 | tf_op jit(solution)/shard_map/all_gather | solution.py:251
  117.9 1.7 layer_step.3
  119.6 28.8 %all_to_all.30 = bf16[16,3,128,128]{3,2,1,0:T(8,128)(2,1)S(1)} all-to-all(bf16[16,3,128,128]{3,2,1,0:T(8,128)(2,1)S(1)} %layer_step.3), channel_id=1, replica_groups=mesh['section'=4,'vertex'=16,'feat'=2] {'vertex'}, dimensions={0} | all-to-all | bytes 3145728 | tf_op jit(solution)/shard_map/all_to_all | solution.py:245
  148.7 1.1 collective-permute-start.3
  149.8 2.2 collective-permute-start.4
  152.0 1.4 collective-permute-start.5
  153.5 1.6 collective-permute-done.4
  155.8 5.4 %all-gather.1 = bf16[8,384,128]{2,1,0:T(8,128)(2,1)S(1)} all-gather(bf16[4,384,128]{2,1,0:T(8,128)(2,1)S(1)} %pad_maximum_fusion.1), channel_id=3, replica_groups=mesh['section'=4,'vertex'=16,'feat'=2] {'feat'}, dimensions={0}, use_global_device_ids=true | all-gather | bytes 1179648 | tf_op jit(solution)/shard_map/all_gather | solution.py:251
  161.2 1.7 layer_step.4
  162.9 24.8 %all_to_all.31 = bf16[16,3,128,128]{3,2,1,0:T(8,128)(2,1)S(1)} all-to-all(bf16[16,3,128,128]{3,2,1,0:T(8,128)(2,1)S(1)} %layer_step.4), channel_id=1, replica_groups=mesh['section'=4,'vertex'=16,'feat'=2] {'vertex'}, dimensions={0} | all-to-all | bytes 3145728 | tf_op jit(solution)/shard_map/all_to_all | solution.py:245
  188.0 1.2 collective-permute-start.6
  189.1 2.7 %collective-permute-start.7 = (bf16[384,128]{1,0:T(8,128)(2,1)S(1)}, bf16[384,128]{1,0:T(8,128)(2,1)S(1)}, u32[]{:S(2)}, u32[]{:S(2)}) collective-permute-start(bf16[384,128]{1,0:T(8,128)(2,1)S(1)} %fusion.26.sup_ref), channel_id=1, source_target_pairs={{0,64},{32,96},{64,0},{96,32},{1,65},{33,97},{65,1},{97,33},{2,66}... | collective-permute-start | bytes 294920 | tf_op jit(solution)/shard_map/ppermute | solution.py:17
  192.7 2.3 collective-permute-done.7
  195.0 1.2 collective-permute-done.8
  196.3 4.5 %all-gather.2 = bf16[8,384,128]{2,1,0:T(8,128)(2,1)S(1)} all-gather(bf16[4,384,128]{2,1,0:T(8,128)(2,1)S(1)} %pad_maximum_fusion.2), channel_id=4, replica_groups=mesh['section'=4,'vertex'=16,'feat'=2] {'feat'}, dimensions={0}, use_global_device_ids=true | all-gather | bytes 1179648 | tf_op jit(solution)/shard_map/all_gather | solution.py:251
  200.9 1.7 layer_step.5
  202.5 1.1 copy-done.2
  203.7 4.4 %all-to-all-start.5 = ((bf16[16,3,128,128]{3,2,1,0:T(8,128)(2,1)}), bf16[16,3,128,128]{3,2,1,0:T(8,128)(2,1)}, u32[]{:S(2)}, u32[]{:S(2)}) async-start(bf16[16,3,128,128]{3,2,1,0:T(8,128)(2,1)} %copy-done.2), calls=%async_computation.5 | async-start | bytes 3145728 | tf_op jit(solution)/shard_map/all_to_all | solution.py:245
  208.6 2.8 %gather_fusion.5 = bf16[4,2,128,512]{3,2,1,0:T(8,128)(2,1)} fusion(bf16[2,4,128,512]{3,2,1,0:T(8,128)(2,1)} %bitcast.151, s32[1024]{0:T(1024)S(1)} %pad_clamp_fusion), kind=kCustom, calls=%fused_computation.2.clone | custom fusion | bytes 2097168 | tf_op jit(solution)/shard_map/jit(_take)/gather | solution.py:237
  211.4 22.6 %collective-permute-done.12 = bf16[1024,512]{1,0:T(8,128)(2,1)} collective-permute-done((bf16[1024,512]{1,0:T(8,128)(2,1)}, bf16[1024,512]{1,0:T(8,128)(2,1)}, u32[]{:S(2)}, u32[]{:S(2)}) %collective-permute-start.12) | collective-permute-done | bytes 1048608 | tf_op jit(solution)/shard_map/ppermute | solution.py:17
  234.0 2.8 %gather_fusion.7 = bf16[4,2,128,512]{3,2,1,0:T(8,128)(2,1)} fusion(bf16[2,4,128,512]{3,2,1,0:T(8,128)(2,1)} %bitcast.55, s32[1024]{0:T(1024)S(1)} %pad_clamp_fusion), kind=kCustom, calls=%fused_computation.6.clone | custom fusion | bytes 2097168 | tf_op jit(solution)/shard_map/jit(_take)/gather | solution.py:237
  236.9 1.8 convert_reduce_fusion
  238.8 1.7 collective-permute-start.10
  240.5 1.0 collective-permute-start.11
  241.5 2.8 %select_bitcast_fusion = (bf16[2,4,128,512]{3,2,0,1:T(8,128)(2,1)}, bf16[2,4,128,512]{3,2,0,1:T(8,128)(2,1)}) fusion(bf16[4,2,128,512]{3,2,1,0:T(8,128)(2,1)S(1)} %copy-done.8, pred[4]{0:T(512)(128)(4,1)S(1)} %compare_and_fusion, bf16[4,2,128,512]{3,2,1,0:T(8,128)(2,1)} %gather_fusion.5), kind=kLoop, calls=%fused_computation.36 | loop fusion | flops 1048576 | bytes 4194308 | tf_op jit(solution)/shard_map/jit(_take)/select_n | solution.py:237
  245.6 4.4 %all-gather.3 = bf16[8,384,128]{2,1,0:T(8,128)(2,1)S(1)} all-gather(bf16[4,384,128]{2,1,0:T(8,128)(2,1)S(1)} %pad_maximum_fusion.3), channel_id=5, replica_groups=mesh['section'=4,'vertex'=16,'feat'=2] {'feat'}, dimensions={0}, use_global_device_ids=true | all-gather | bytes 1179648 | tf_op jit(solution)/shard_map/all_gather | solution.py:251
  252.6 1.1 multiply_bitcast_fusion
  253.8 2.6 fusion.11
  256.4 5.6 %fusion.1 = bf16[1,2048,512]{2,1,0:T(8,128)(2,1)} fusion(bf16[1,2048,512]{2,1,0:T(8,128)(2,1)} %param.15, pred[2048]{0:T(1024)(128)(4,1)S(1)} %get-tuple-element.18, s32[384]{0:T(512)S(1)} %bitcast.171, bf16[384,512]{1,0:T(8,128)(2,1)S(1)} %broadcast_select_fusion, bf16[2,4,128,512]{3,2,0,1:T(8,128)(2,1)} %get-tuple-element.22, ...), kind=kOutput, calls=%fused_computation.18 | convolution fusion | flops 1211826176 | bytes 7212549 | tf_op jit(solution)/shard_map/dot_general | solution.py:279
  (98 shorter events, 15.3 us)
Async XLA Ops:
  0.6 27.1 %copy-start = (bf16[2048,512]{1,0:T(8,128)(2,1)S(1)}, bf16[2048,512]{1,0:T(8,128)(2,1)}, u32[]{:S(2)}) copy-start(bf16[2048,512]{1,0:T(8,128)(2,1)} %param.14) | copy-start | bytes 6291460
  3.1 19.0 %all-to-all-start.2 = ((bf16[4,1024,128]{1,2,0:T(8,128)(2,1)}), bf16[4,1024,128]{1,2,0:T(8,128)(2,1)S(1)}, u32[]{:S(2)}, u32[]{:S(2)}) async-start(bf16[4,1024,128]{1,2,0:T(8,128)(2,1)} %bitcast.12), calls=%async_computation.2 | async-start | bytes 2097152 | tf_op jit(solution)/shard_map/all_to_all | solution.py:215
  11.8 4.0 %copy-start.17 = (s32[3,128]{1,0:T(4,128)S(1)}, s32[3,128]{1,0:T(4,128)}, u32[]{:S(2)}) copy-start(s32[3,128]{1,0:T(4,128)} %param.21) | copy-start | bytes 4612
  22.1 1.0 copy-start.9
  23.1 29.0 %all-to-all-start = ((bf16[4,2048,128]{2,1,0:T(8,128)(2,1)}), bf16[4,2048,128]{2,1,0:T(8,128)(2,1)}, u32[]{:S(2)}, u32[]{:S(2)}) async-start(bf16[4,2048,128]{2,1,0:T(8,128)(2,1)} %bitcast.148), calls=%async_computation | async-start | bytes 4194304 | tf_op jit(solution)/shard_map/all_to_all | solution.py:214
  27.6 2.2 copy-start.5
  27.6 2.2 copy-start.6
  27.6 2.2 copy-start.7
  29.8 2.8 %copy-start.3 = (bf16[3,64,128,128]{3,2,1,0:T(8,128)(2,1)S(1)}, bf16[3,64,128,128]{3,2,1,0:T(8,128)(2,1)}, u32[]{:S(2)}) copy-start(bf16[3,64,128,128]{3,2,1,0:T(8,128)(2,1)} %values_ref.1) | copy-start | bytes 18874372
  42.4 1.2 copy-start.10
  67.1 36.0 %all-to-all-start.1 = ((bf16[16,3,128,128]{3,2,1,0:T(8,128)(2,1)}), bf16[16,3,128,128]{3,2,1,0:T(8,128)(2,1)}, u32[]{:S(2)}, u32[]{:S(2)}) async-start(bf16[16,3,128,128]{3,2,1,0:T(8,128)(2,1)} %first_partial.1), calls=%async_computation.1 | async-start | bytes 3145728 | tf_op jit(solution)/shard_map/all_to_all | solution.py:245
  74.9 1.4 copy-start.4
  104.8 7.4 %collective-permute-start = (bf16[384,128]{1,0:T(8,128)(2,1)S(1)}, bf16[384,128]{1,0:T(8,128)(2,1)S(1)}, u32[]{:S(2)}, u32[]{:S(2)}) collective-permute-start(bf16[384,128]{1,0:T(8,128)(2,1)S(1)} %fusion.28.sup_ref), channel_id=1, source_target_pairs={{0,32},{32,64},{64,96},{96,0},{1,33},{33,65},{65,97},{97,1},{2,34}... | collective-permute-start | bytes 294920 | tf_op jit(solution)/shard_map/ppermute | solution.py:17
  105.2 7.0 %collective-permute-start.1 = (bf16[384,128]{1,0:T(8,128)(2,1)S(1)}, bf16[384,128]{1,0:T(8,128)(2,1)S(1)}, u32[]{:S(2)}, u32[]{:S(2)}) collective-permute-start(bf16[384,128]{1,0:T(8,128)(2,1)S(1)} %fusion.28.sup_ref), channel_id=1, source_target_pairs={{0,64},{32,96},{64,0},{96,32},{1,65},{33,97},{65,1},{97,33},{2,66}... | collective-permute-start | bytes 294920 | tf_op jit(solution)/shard_map/ppermute | solution.py:17
  107.0 5.3 %collective-permute-start.2 = (bf16[384,128]{1,0:T(8,128)(2,1)S(1)}, bf16[384,128]{1,0:T(8,128)(2,1)S(1)}, u32[]{:S(2)}, u32[]{:S(2)}) collective-permute-start(bf16[384,128]{1,0:T(8,128)(2,1)S(1)} %fusion.28.sup_ref), channel_id=1, source_target_pairs={{0,96},{32,0},{64,32},{96,64},{1,97},{33,1},{65,33},{97,65},{2,98}... | collective-permute-start | bytes 294920 | tf_op jit(solution)/shard_map/ppermute | solution.py:17
  107.7 10.3 %slice-start = ((s8[4718592]{0:T(1024)(128)(4,1)}), s8[4194304]{0:T(1024)(128)(4,1)S(1)}, s32[]{:S(2)}) async-start(s8[4718592]{0:T(1024)(128)(4,1)} %bitcast.133), calls=%async_computation.6 | async-start | bytes 8388608
  107.7 10.3 %slice-start.1 = ((s8[4718592]{0:T(1024)(128)(4,1)}), s8[524288]{0:T(1024)(128)(4,1)S(1)}, s32[]{:S(2)}) async-start(s8[4718592]{0:T(1024)(128)(4,1)} %bitcast.133), calls=%async_computation.7 | async-start | bytes 1048576
  119.6 33.8 %copy-start.16 = (bf16[2,4,128,128]{3,2,0,1:T(8,128)(2,1)S(1)}, bf16[2,4,128,128]{3,2,0,1:T(8,128)(2,1)}, u32[]{:S(2)}) copy-start(bf16[2,4,128,128]{3,2,0,1:T(8,128)(2,1)} %get-tuple-element.25) | copy-start | bytes 786436
  148.7 4.7 %collective-permute-start.3 = (bf16[384,128]{1,0:T(8,128)(2,1)S(1)}, bf16[384,128]{1,0:T(8,128)(2,1)S(1)}, u32[]{:S(2)}, u32[]{:S(2)}) collective-permute-start(bf16[384,128]{1,0:T(8,128)(2,1)S(1)} %fusion.27.sup_ref), channel_id=1, source_target_pairs={{0,32},{32,64},{64,96},{96,0},{1,33},{33,65},{65,97},{97,1},{2,34}... | collective-permute-start | bytes 294920 | tf_op jit(solution)/shard_map/ppermute | solution.py:17
  149.8 5.3 %collective-permute-start.4 = (bf16[384,128]{1,0:T(8,128)(2,1)S(1)}, bf16[384,128]{1,0:T(8,128)(2,1)S(1)}, u32[]{:S(2)}, u32[]{:S(2)}) collective-permute-start(bf16[384,128]{1,0:T(8,128)(2,1)S(1)} %fusion.27.sup_ref), channel_id=1, source_target_pairs={{0,64},{32,96},{64,0},{96,32},{1,65},{33,97},{65,1},{97,33},{2,66}... | collective-permute-start | bytes 294920 | tf_op jit(solution)/shard_map/ppermute | solution.py:17
  152.0 3.8 %collective-permute-start.5 = (bf16[384,128]{1,0:T(8,128)(2,1)S(1)}, bf16[384,128]{1,0:T(8,128)(2,1)S(1)}, u32[]{:S(2)}, u32[]{:S(2)}) collective-permute-start(bf16[384,128]{1,0:T(8,128)(2,1)S(1)} %fusion.27.sup_ref), channel_id=1, source_target_pairs={{0,96},{32,0},{64,32},{96,64},{1,97},{33,1},{65,33},{97,65},{2,98}... | collective-permute-start | bytes 294920 | tf_op jit(solution)/shard_map/ppermute | solution.py:17
  162.9 29.4 %copy-start.15 = (bf16[2,4,128,128]{3,2,0,1:T(8,128)(2,1)S(1)}, bf16[2,4,128,128]{3,2,0,1:T(8,128)(2,1)}, u32[]{:S(2)}) copy-start(bf16[2,4,128,128]{3,2,0,1:T(8,128)(2,1)} %get-tuple-element.24) | copy-start | bytes 786436
  188.0 4.7 %collective-permute-start.6 = (bf16[384,128]{1,0:T(8,128)(2,1)S(1)}, bf16[384,128]{1,0:T(8,128)(2,1)S(1)}, u32[]{:S(2)}, u32[]{:S(2)}) collective-permute-start(bf16[384,128]{1,0:T(8,128)(2,1)S(1)} %fusion.26.sup_ref), channel_id=1, source_target_pairs={{0,32},{32,64},{64,96},{96,0},{1,33},{33,65},{65,97},{97,1},{2,34}... | collective-permute-start | bytes 294920 | tf_op jit(solution)/shard_map/ppermute | solution.py:17
  189.1 5.9 %collective-permute-start.7 = (bf16[384,128]{1,0:T(8,128)(2,1)S(1)}, bf16[384,128]{1,0:T(8,128)(2,1)S(1)}, u32[]{:S(2)}, u32[]{:S(2)}) collective-permute-start(bf16[384,128]{1,0:T(8,128)(2,1)S(1)} %fusion.26.sup_ref), channel_id=1, source_target_pairs={{0,64},{32,96},{64,0},{96,32},{1,65},{33,97},{65,1},{97,33},{2,66}... | collective-permute-start | bytes 294920 | tf_op jit(solution)/shard_map/ppermute | solution.py:17
  191.9 4.4 %collective-permute-start.8 = (bf16[384,128]{1,0:T(8,128)(2,1)S(1)}, bf16[384,128]{1,0:T(8,128)(2,1)S(1)}, u32[]{:S(2)}, u32[]{:S(2)}) collective-permute-start(bf16[384,128]{1,0:T(8,128)(2,1)S(1)} %fusion.26.sup_ref), channel_id=1, source_target_pairs={{0,96},{32,0},{64,32},{96,64},{1,97},{33,1},{65,33},{97,65},{2,98}... | collective-permute-start | bytes 294920 | tf_op jit(solution)/shard_map/ppermute | solution.py:17
  202.5 1.1 copy-start.2
  203.7 33.2 %all-to-all-start.5 = ((bf16[16,3,128,128]{3,2,1,0:T(8,128)(2,1)}), bf16[16,3,128,128]{3,2,1,0:T(8,128)(2,1)}, u32[]{:S(2)}, u32[]{:S(2)}) async-start(bf16[16,3,128,128]{3,2,1,0:T(8,128)(2,1)} %copy-done.2), calls=%async_computation.5 | async-start | bytes 3145728 | tf_op jit(solution)/shard_map/all_to_all | solution.py:245
  208.1 26.0 %collective-permute-start.12 = (bf16[1024,512]{1,0:T(8,128)(2,1)}, bf16[1024,512]{1,0:T(8,128)(2,1)}, u32[]{:S(2)}, u32[]{:S(2)}) collective-permute-start(bf16[1024,512]{1,0:T(8,128)(2,1)} %bitcast.150), channel_id=1, source_target_pairs={{0,32},{32,64},{64,96},{96,0},{1,33},{33,65},{65,97},{97,1},{2,34}... | collective-permute-start | bytes 3145736 | tf_op jit(solution)/shard_map/ppermute | solution.py:17
  236.9 4.6 %copy-start.8 = (bf16[4,2,128,512]{3,2,1,0:T(8,128)(2,1)S(1)}, bf16[4,2,128,512]{3,2,1,0:T(8,128)(2,1)}, u32[]{:S(2)}) copy-start(bf16[4,2,128,512]{3,2,1,0:T(8,128)(2,1)} %gather_fusion.7) | copy-start | bytes 3145732
  238.7 6.2 %collective-permute-start.9 = (bf16[384,128]{1,0:T(8,128)(2,1)S(1)}, bf16[384,128]{1,0:T(8,128)(2,1)S(1)}, u32[]{:S(2)}, u32[]{:S(2)}) collective-permute-start(bf16[384,128]{1,0:T(8,128)(2,1)S(1)} %fusion.25), channel_id=1, source_target_pairs={{0,32},{32,64},{64,96},{96,0},{1,33},{33,65},{65,97},{97,1},{2,34}... | collective-permute-start | bytes 294920 | tf_op jit(solution)/shard_map/ppermute | solution.py:17
  238.8 6.1 %collective-permute-start.10 = (bf16[384,128]{1,0:T(8,128)(2,1)S(1)}, bf16[384,128]{1,0:T(8,128)(2,1)S(1)}, u32[]{:S(2)}, u32[]{:S(2)}) collective-permute-start(bf16[384,128]{1,0:T(8,128)(2,1)S(1)} %fusion.25), channel_id=1, source_target_pairs={{0,64},{32,96},{64,0},{96,32},{1,65},{33,97},{65,1},{97,33},{2,66}... | collective-permute-start | bytes 294920 | tf_op jit(solution)/shard_map/ppermute | solution.py:17
  240.5 5.1 %collective-permute-start.11 = (bf16[384,128]{1,0:T(8,128)(2,1)S(1)}, bf16[384,128]{1,0:T(8,128)(2,1)S(1)}, u32[]{:S(2)}, u32[]{:S(2)}) collective-permute-start(bf16[384,128]{1,0:T(8,128)(2,1)S(1)} %fusion.25), channel_id=1, source_target_pairs={{0,96},{32,0},{64,32},{96,64},{1,97},{33,1},{65,33},{97,65},{2,98}... | collective-permute-start | bytes 294920 | tf_op jit(solution)/shard_map/ppermute | solution.py:17
  250.2 0.9 copy-start.11
  250.2 1.1 copy-start.13
  251.4 2.4 copy-start.14
  253.8 2.6 %copy-start.12 = (bf16[2,4,384,128]{3,2,1,0:T(8,128)(2,1)S(1)}, bf16[2,4,384,128]{3,2,1,0:T(8,128)(2,1)}, u32[]{:S(2)}) copy-start(bf16[2,4,384,128]{3,2,1,0:T(8,128)(2,1)} %copy-done.11) | copy-start | bytes 2359300
  256.4 5.6 %copy-start.1 = (bf16[2048,512]{1,0:T(8,128)(2,1)S(1)}, bf16[2048,512]{1,0:T(8,128)(2,1)}, u32[]{:S(2)}) copy-start(bf16[2048,512]{1,0:T(8,128)(2,1)} %param.14) | copy-start | bytes 6291460
where the time goes:
time: 263 us; the launch traced here: 262 us
  blocking collectives  73.5 us (28%)
  Pallas kernels  54.4 us (21%)
  waiting for transfers between devices  39.1 us (15%)
  local copies, waits for them, and re-layouts  36.8 us (14%)
  starting transfers between devices  36.4 us (14%)
  other arithmetic  12.3 us (5%)
  matrix products  8.18 us (3%)
    all_to_all x2, blocking collectives, shards(): arrived = lax.all_to_all(partial, 'vertex', 0, 0, tiled=True)  53.5 us
    ppermute x13, waiting for transfers between devices, rotated(): lax.ppermute(array, axis, [(i, (i + by) % devices) for i in range(devices)])  30.2 us
    pallas_call x1, Pallas kernels, static_parts(): pl.pallas_call(kernel, out_shape=(jax.ShapeDtypeStruct((later, spans, row...  26.7 us
    all_gather x4, blocking collectives, shards(): gathered = lax.all_gather(near, 'feat', axis=0)  19.9 us
    ppermute x13, starting transfers between devices, rotated(): lax.ppermute(array, axis, [(i, (i + by) % devices) for i in range(devices)])  14.9 us
    unnamed x42, local copies, waits for them, and re-layouts  14.7 us
    pallas_call x1, Pallas kernels, first_partial(): pl.pallas_call(kernel, out_shape=jax.ShapeDtypeStruct((row_devices, spans...  12.9 us
    all_to_all x2, starting transfers between devices, shards(): arrived = lax.all_to_all(partial, 'vertex', 0, 0, tiled=True)  12.2 us
  transfers between devices with their start and end apart: 17, of which 10 were waited for; matrix products, arithmetic and copies ran while one was open for 11% of the time, Pallas kernels for 14%

commit v1 on v0

v1 whole, which is shorter than its diff:
```python
import math

import jax
import jax.numpy as jnp
from jax import lax
from jax.experimental import pallas as pl
from jax.experimental.pallas import tpu as pltpu
from jax.sharding import PartitionSpec as P

RESIDUAL_SHARE = 0.2
BETA_SCALE = 0.5
MIB = 1 << 20
CHUNKS = ((0, 3),)
ROW_CHUNK = 512


def rotated(array, axis, by):
    devices = lax.axis_size(axis)
    return lax.ppermute(array, axis, [(i, (i + by) % devices) for i in range(devices)])


def after(array, earlier):
    return lax.optimization_barrier((array, earlier))[0]


def vmem_params(mib):
    return pltpu.CompilerParams(vmem_limit_bytes=mib * MIB)


def cost(flops, bytes_accessed):
    return pl.CostEstimate(flops=flops, transcendentals=0, bytes_accessed=bytes_accessed)


def dense_adjacency(tile_values, tile_rows, tile_cols, tile_counts, row_blocks, col_blocks):
    spans, slots, side, _ = tile_values.shape
    rows, cols = row_blocks * side, col_blocks * side

    def kernel(rows_ref, cols_ref, counts_ref, values_ref, out_ref):
        span = pl.program_id(0)
        out_ref[...] = jnp.zeros_like(out_ref)

        @pl.loop(0, counts_ref[span])
        def _(slot):
            row = pl.multiple_of(rows_ref[span, slot] * side, side)
            col = pl.multiple_of(cols_ref[span, slot] * side, side)
            out_ref[0, pl.ds(row, side), pl.ds(col, side)] = values_ref[0, slot]

    return pl.pallas_call(
        kernel,
        out_shape=jax.ShapeDtypeStruct((spans, rows, cols), jnp.bfloat16),
        grid_spec=pltpu.PrefetchScalarGridSpec(
            num_scalar_prefetch=3,
            grid=(spans,),
            in_specs=[pl.BlockSpec((1, slots, side, side), lambda c, *_: (c, 0, 0, 0))],
            out_specs=pl.BlockSpec((1, rows, cols), lambda c, *_: (c, 0, 0)),
        ),
        compiler_params=vmem_params(40),
        cost_estimate=cost(0, 2 * spans * (rows * cols + slots * side * side)),
        name="dense_adjacency",
    )(tile_rows, tile_cols, tile_counts[:, 0], tile_values)


def first_partial(adjacency, hist, feats, replaced, row_devices, begin, end):
    _, rows, cols = adjacency.shape
    spans = end - begin
    width = hist.shape[1]
    rows_local = rows // row_devices
    step = ROW_CHUNK // rows_local

    def kernel(adj_ref, hist_ref, feat_ref, mask_ref, out_ref, table):
        @pl.when(pl.program_id(1) == 0)
        def _():
            table[...] = jnp.where(mask_ref[0] > 0, feat_ref[...], hist_ref[...])

        part = jnp.dot(adj_ref[0], table[...], preferred_element_type=jnp.float32)
        out_ref[:, 0] = part.astype(jnp.bfloat16).reshape(step, rows_local, width)

    return pl.pallas_call(
        kernel,
        out_shape=jax.ShapeDtypeStruct((row_devices, spans, rows_local, width), jnp.bfloat16),
        grid=(spans, rows // ROW_CHUNK),
        in_specs=[
            pl.BlockSpec((1, ROW_CHUNK, cols), lambda c, m: (c + begin, m, 0)),
            pl.BlockSpec((cols, width), lambda c, m: (0, 0)),
            pl.BlockSpec((cols, width), lambda c, m: (0, 0)),
            pl.BlockSpec((1, cols, width), lambda c, m: (c + begin, 0, 0)),
        ],
        out_specs=pl.BlockSpec((step, 1, rows_local, width), lambda c, m: (m, c, 0, 0)),
        scratch_shapes=[pltpu.VMEM((cols, width), jnp.bfloat16)],
        compiler_params=vmem_params(24),
        cost_estimate=cost(
            2 * spans * rows * cols * width, 2 * spans * (rows * cols + rows * width)
        ),
        name="first_partial",
    )(adjacency, hist, feats, replaced)


def replaced_columns(adjacency, select, begin, end):
    _, rows, cols = adjacency.shape
    spans = end - begin
    picks = select.shape[1]

    def kernel(adj_ref, sel_ref, out_ref):
        out_ref[0] = jnp.dot(
            adj_ref[0], sel_ref[...], preferred_element_type=jnp.float32
        ).astype(jnp.bfloat16)

    return pl.pallas_call(
        kernel,
        out_shape=jax.ShapeDtypeStruct((spans, rows, picks), jnp.bfloat16),
        grid=(spans, rows // ROW_CHUNK),
        in_specs=[
            pl.BlockSpec((1, ROW_CHUNK, cols), lambda c, m: (c + begin, m, 0)),
            pl.BlockSpec((cols, picks), lambda c, m: (0, 0)),
        ],
        out_specs=pl.BlockSpec((1, ROW_CHUNK, picks), lambda c, m: (c, m, 0)),
        compiler_params=vmem_params(24),
        cost_estimate=cost(2 * spans * rows * cols * picks, 2 * spans * rows * (cols + picks)),
        name="replaced_columns",
    )(adjacency, select)


def static_parts(adjacency, hist_slices, replaced, begin, end):
    _, rows, cols = adjacency.shape
    spans = end - begin
    layers, _, width = hist_slices.shape
    later = layers - 1

    def kernel(adj_ref, hist_ref, mask_ref, static_ref, right):
        @pl.when(pl.program_id(1) == 0)
        def _():
            for layer in range(later):
                right[:, layer * width : (layer + 1) * width] = jnp.where(
                    mask_ref[0] > 0, jnp.zeros_like(hist_ref[0]), hist_ref[layer + 1]
                )

        part = jnp.dot(adj_ref[0], right[...], preferred_element_type=jnp.float32)
        for layer in range(later):
            static_ref[layer, 0] = part[:, layer * width : (layer + 1) * width]

    return pl.pallas_call(
        kernel,
        out_shape=jax.ShapeDtypeStruct((later, spans, rows, width), jnp.float32),
        grid=(spans, rows // ROW_CHUNK),
        in_specs=[
            pl.BlockSpec((1, ROW_CHUNK, cols), lambda c, m: (c + begin, m, 0)),
            pl.BlockSpec((layers, cols, width), lambda c, m: (0, 0, 0)),
            pl.BlockSpec((1, cols, width), lambda c, m: (c + begin, 0, 0)),
        ],
        out_specs=pl.BlockSpec((later, 1, ROW_CHUNK, width), lambda c, m: (0, c, m, 0)),
        scratch_shapes=[pltpu.VMEM((cols, later * width), jnp.bfloat16)],
        compiler_params=vmem_params(32),
        cost_estimate=cost(
            2 * spans * rows * cols * later * width,
            spans * (2 * rows * cols + 4 * later * rows * width),
        ),
        name="static_parts",
    )(adjacency, hist_slices, replaced)


def fill_left(left, gath_ref, section, halves, parts, width):
    for half in range(halves):
        for part in range(parts):
            first = (half * parts + part) * width
            place = lax.rem(section - part + parts, parts)
            left[:, first : first + width] = gath_ref[half, place]


def layer_step(place, gathered, support, slices, statics, columns, fresh_before, layer, beta, row_devices, begin):
    halves, parts, picks, width = gathered.shape
    spans, rows, every = columns.shape
    rows_local = rows // row_devices
    depth = halves * parts * width
    used_before = begin * rows_local
    step = 4

    def kernel(place_ref, gath_ref, sup_ref, w_ref, static_ref, cols_ref, *refs):
        if begin:
            before_ref, fresh_ref, out_ref, left, known = refs
            known[:used_before] = before_ref[...]
        else:
            fresh_ref, out_ref, left, known = refs
        fill_left(left, gath_ref, place_ref[0], halves, parts, width)
        projected = jnp.dot(left[...], w_ref[0], preferred_element_type=jnp.float32)
        fresh = jnp.maximum(
            (1.0 - beta) * sup_ref[...].astype(jnp.float32) + beta * projected, 0.0
        ).astype(jnp.bfloat16)
        known[used_before:] = fresh
        fresh_ref[...] = known[...]
        for span in range(spans):
            used = (begin + span + 1) * rows_local
            right = known[:used]
            for first in range(0, row_devices, step):
                at = slice(first * rows_local, (first + step) * rows_local)
                part = static_ref[0, span, at] + jnp.dot(
                    cols_ref[span, at, :used], right, preferred_element_type=jnp.float32
                )
                out_ref[first : first + step, span] = part.astype(jnp.bfloat16).reshape(
                    step, rows_local, width
                )

    whole = used_before + picks
    operands = [gathered, support, slices, statics, columns]
    specs = [
        pl.BlockSpec(gathered.shape, lambda i, p: (0, 0, 0, 0)),
        pl.BlockSpec(support.shape, lambda i, p: (0, 0)),
        pl.BlockSpec((1, depth, width), lambda i, p: (lax.rem(p[0] - layer + parts, parts), 0, 0)),
        pl.BlockSpec((1, spans, rows, width), lambda i, p: (layer, 0, 0, 0)),
        pl.BlockSpec(columns.shape, lambda i, p: (0, 0, 0)),
    ]
    if begin:
        operands.append(fresh_before)
        specs.append(pl.BlockSpec(fresh_before.shape, lambda i, p: (0, 0)))
    return pl.pallas_call(
        kernel,
        out_shape=(
            jax.ShapeDtypeStruct((whole, width), jnp.bfloat16),
            jax.ShapeDtypeStruct((row_devices, spans, rows_local, width), jnp.bfloat16),
        ),
        grid_spec=pltpu.PrefetchScalarGridSpec(
            num_scalar_prefetch=1,
            grid=(1,),
            in_specs=specs,
            out_specs=(
                pl.BlockSpec((whole, width), lambda i, p: (0, 0)),
                pl.BlockSpec((row_devices, spans, rows_local, width), lambda i, p: (0, 0, 0, 0)),
            ),
            scratch_shapes=[
                pltpu.VMEM((picks, depth), jnp.bfloat16),
                pltpu.VMEM((whole, width), jnp.bfloat16),
            ],
        ),
        compiler_params=vmem_params(40),
        cost_estimate=cost(
            2 * picks * depth * width + 2 * spans * rows * width * every,
            6 * spans * rows * width + 2 * spans * rows * every,
        ),
        name="layer_step",
    )(place, *operands)


def whole_rows(place, betas, gathered, weight_cols, earlier, layer):
    halves, parts, picks, width = gathered.shape
    depth, half = weight_cols.shape

    def kernel(place_ref, betas_ref, gath_ref, w_ref, *refs):
        if layer:
            earlier_ref, out_ref, left, own = refs
        else:
            out_ref, left, own = refs
        section, feat = place_ref[0], place_ref[1]

        @pl.when(section == layer)
        def _():
            beta = betas_ref[layer]
            fill_left(left, gath_ref, section, halves, parts, width)
            for part in range(parts):
                own[:, part * width : (part + 1) * width] = gath_ref[
                    feat, lax.rem(section - part + parts, parts)
                ]
            projected = jnp.dot(left[...], w_ref[...], preferred_element_type=jnp.float32)
            out_ref[...] = jnp.maximum(
                (1.0 - beta) * own[...].astype(jnp.float32) + beta * projected, 0.0
            ).astype(jnp.bfloat16)

        @pl.when(section != layer)
        def _():
            out_ref[...] = earlier_ref[...] if layer else jnp.zeros_like(out_ref)

    operands = [gathered, weight_cols] + ([earlier] if layer else [])
    specs = [
        pl.BlockSpec(gathered.shape, lambda i, *_: (0, 0, 0, 0)),
        pl.BlockSpec(weight_cols.shape, lambda i, *_: (0, 0)),
    ] + ([pl.BlockSpec((picks, half), lambda i, *_: (0, 0))] if layer else [])
    return pl.pallas_call(
        kernel,
        out_shape=jax.ShapeDtypeStruct((picks, half), jnp.bfloat16),
        grid_spec=pltpu.PrefetchScalarGridSpec(
            num_scalar_prefetch=2,
            grid=(1,),
            in_specs=specs,
            out_specs=pl.BlockSpec((picks, half), lambda i, *_: (0, 0)),
            scratch_shapes=[
                pltpu.VMEM((picks, depth), jnp.bfloat16),
                pltpu.VMEM((picks, half), jnp.bfloat16),
            ],
        ),
        compiler_params=vmem_params(24),
        cost_estimate=cost(2 * picks * depth * half, 2 * (picks * depth + depth * half)),
        name="whole_rows",
    )(place, betas, *operands)


def replace_rows(stored, ids, fresh):
    owned, half = stored.shape
    picks = ids.shape[1]
    chunk = 512

    def kernel(stored_ref, ids_ref, fresh_ref, out_ref):
        first = pl.program_id(0) * chunk
        vertex = first + lax.broadcasted_iota(jnp.int32, (chunk, picks), 0)
        hits = (vertex == ids_ref[...]).astype(jnp.float32)
        placed = jnp.dot(
            hits.astype(jnp.bfloat16), fresh_ref[...], preferred_element_type=jnp.float32
        )
        found = jnp.sum(hits, axis=1, keepdims=True) > 0
        out_ref[...] = jnp.where(found, placed, stored_ref[...].astype(jnp.float32)).astype(
            jnp.bfloat16
        )

    return pl.pallas_call(
        kernel,
        out_shape=jax.ShapeDtypeStruct((owned, half), jnp.bfloat16),
        grid=(owned // chunk,),
        in_specs=[
            pl.BlockSpec((chunk, half), lambda i: (i, 0)),
            pl.BlockSpec((1, picks), lambda i: (0, 0)),
            pl.BlockSpec((picks, half), lambda i: (0, 0)),
        ],
        out_specs=pl.BlockSpec((chunk, half), lambda i: (i, 0)),
        compiler_params=vmem_params(24),
        cost_estimate=cost(2 * owned * picks * half, 4 * owned * half),
        name="replace_rows",
    )(stored, ids, fresh)


def shards(features, history, weights, tile_values, tile_rows, tile_cols, tile_counts, span_ids):
    spans, rows_local = span_ids.shape
    side = tile_values.shape[2]
    owned, half = features.shape
    layers = lax.axis_size("section")
    row_devices = lax.axis_size("vertex")
    section = lax.axis_index("section")
    width = half // layers
    picks = spans * rows_local
    depth = weights.shape[1]
    betas = [math.log(BETA_SCALE / (layer + 1) + 1.0) for layer in range(layers)]
    place = jnp.stack([section, lax.axis_index("feat")]).astype(jnp.int32)
    beta_table = jnp.array(betas, jnp.float32)

    stored = history[0]
    by_section = jnp.stack([stored[:, i * width : (i + 1) * width] for i in range(layers)])
    hist_slices = lax.all_to_all(by_section, "section", 0, 0, tiled=True)

    ids = span_ids.reshape(1, picks)
    hits = jnp.arange(owned)[:, None] == ids
    select = hits.astype(jnp.bfloat16)
    upto = jnp.stack([jnp.any(hits[:, : (c + 1) * rows_local], axis=1) for c in range(spans)])
    replaced = jnp.broadcast_to(upto[:, :, None], (spans, owned, width)).astype(jnp.bfloat16)
    feat_slice = lax.dynamic_slice_in_dim(features, section * width, width, 1)
    initial_half = jnp.take(features, ids[0], axis=0)
    initial = lax.dynamic_slice_in_dim(initial_half, section * width, width, 1).astype(jnp.float32)
    adjacency = dense_adjacency(
        tile_values, tile_rows, tile_cols, tile_counts, rows_local * row_devices // side, owned // side
    )
    columns = [replaced_columns(adjacency, select, begin, end) for begin, end in CHUNKS]

    partials = [
        first_partial(adjacency, hist_slices[0], feat_slice, replaced, row_devices, begin, end)
        for begin, end in CHUNKS
    ]
    own_weights = after(weights[0], partials)
    late_slices = after(hist_slices, partials)
    statics = [static_parts(adjacency, late_slices, replaced, begin, end) for begin, end in CHUNKS]
    by_distance = [
        lax.dynamic_slice_in_dim(own_weights, (section + by) % layers * width, width, 1)
        for by in range(layers)
    ]
    weight_slices = jnp.stack(
        [by_distance[0]] + [rotated(by_distance[by], "section", by) for by in range(1, layers)]
    )

    rows_kept = [None] * len(CHUNKS)
    table = None
    for layer in range(layers):
        fresh = None
        if layer == layers - 1:
            before = rotated(jnp.concatenate(rows_kept, axis=0), "section", 1)
            table = replace_rows(stored, ids, jnp.where(section == 0, initial_half, before))
        for index, (begin, end) in enumerate(CHUNKS):
            mine = slice(begin * rows_local, end * rows_local)
            arrived = lax.all_to_all(partials[index], "vertex", 0, 0, tiled=True)
            if table is not None:
                arrived, table = lax.optimization_barrier((arrived, table))
            aggregate = jnp.sum(arrived.astype(jnp.float32), axis=0).reshape(-1, width)
            support = (
                (1.0 - RESIDUAL_SHARE) * aggregate + RESIDUAL_SHARE * initial[mine]
            ).astype(jnp.bfloat16)
            near = jnp.stack(
                [support] + [rotated(support, "section", by) for by in range(1, layers)]
            )
            gathered = lax.all_gather(near, "feat", axis=0)
            if layer < layers - 1:
                fresh, partials[index] = layer_step(
                    place,
                    gathered,
                    support,
                    weight_slices,
                    statics[index],
                    columns[index],
                    fresh,
                    layer,
                    betas[layer],
                    row_devices,
                    begin,
                )
            rows_kept[index] = whole_rows(
                place, beta_table, gathered, own_weights, rows_kept[index], layer
            )
    rows_out = jnp.concatenate(rows_kept, axis=0)
    return (rows_out.reshape(1, spans, rows_local, half), table[None])


def solution(mesh):
    placed = (
        P("vertex", "feat"),
        P("section", "vertex", "feat"),
        P("section", None, "feat"),
        P(None, "vertex", None, None),
        P(None, "vertex"),
        P(None, "vertex"),
        P(None, "vertex"),
        P(None, "vertex"),
    )
    return jax.shard_map(
        shards,
        mesh=mesh,
        in_specs=placed,
        out_specs=(P("section", None, "vertex", "feat"), P("section", "vertex", "feat")),
        check_vma=False,
    )
```

time: 263 us -> 264 us (level)
  Pallas kernels: 54.4 us -> 78.6 us
  matrix products: 8.18 us -> 0 us
  local copies, waits for them, and re-layouts: 36.8 us -> 28.7 us
  starting transfers between devices: 36.4 us -> 29.8 us
    pallas_call x4 -> x10, Pallas kernels: 31.7 us -> 58.9 us  [the longest x1 21.2 us: static_parts(): pl.pallas_call(kernel, out_shape=jax.ShapeDtypeStruct((later, spans, rows...]
    gather x8 -> x1, local copies, waits for them, and re-layouts: 10.7 us -> 2.06 us  [shards(): initial_half = jnp.take(features, ids[0], axis=0)]
    dot_general x2 -> x0, matrix products: 8.18 us -> none  [the longest x1 5.56 us: shards(): jnp.dot(select, fresh, preferred_element_type=jnp.float32)]
    unnamed x42 -> x45, local copies, waits for them, and re-layouts: 14.7 us -> 21.6 us
    squeeze x2 -> x0, local copies, waits for them, and re-layouts: 4.58 us -> none  [the longest x1 4.53 us: shards(): statics[layer]]
    all_to_all x4 -> x3, starting transfers between devices: 21.6 us -> 17.3 us  [the longest x2 12.3 us: shards(): arrived = lax.all_to_all(partials[index], 'vertex', 0, 0, tiled=True)]
    pallas_call x1, Pallas kernels: 12.9 us -> 9.45 us  [first_partial(): pl.pallas_call(kernel, out_shape=jax.ShapeDtypeStruct((row_devices, spans...]
    another operation x0 -> x3, other arithmetic: none -> 2.9 us  [the longest x1 1.58 us: shards(): jnp.stack([stored[:, i * width:(i + 1) * width] for i in range(layers)])]
  transfers between devices with their start and end apart: 17 -> 19, of which waited for: 10 -> 14; matrix products, arithmetic and copies ran while one was open for 11% -> 4% of each run, Pallas kernels for 14% -> 21%
where the time goes in v1:
time: 264 us; the launch traced here: 262 us
  Pallas kernels  78.6 us (30%)
  blocking collectives  74.6 us (28%)
  waiting for transfers between devices  37.3 us (14%)
  starting transfers between devices  29.8 us (11%)
  local copies, waits for them, and re-layouts  28.7 us (11%)
  other arithmetic  12.1 us (5%)
    all_to_all x2, blocking collectives, shards(): arrived = lax.all_to_all(partials[index], 'vertex', 0, 0, tiled=True)  53.4 us
    ppermute x16, waiting for transfers between devices, rotated(): lax.ppermute(array, axis, [(i, (i + by) % devices) for i in range(devices)])  30.3 us
    unnamed x45, local copies, waits for them, and re-layouts  21.6 us
    pallas_call x1, Pallas kernels, static_parts(): pl.pallas_call(kernel, out_shape=jax.ShapeDtypeStruct((later, spans, rows...  21.2 us
    all_gather x4, blocking collectives, shards(): gathered = lax.all_gather(near, 'feat', axis=0)  21.2 us
    pallas_call x1, Pallas kernels, replaced_columns(): pl.pallas_call(kernel, out_shape=jax.ShapeDtypeStruct((spans, rows, picks...  18.7 us
    ppermute x16, starting transfers between devices, rotated(): lax.ppermute(array, axis, [(i, (i + by) % devices) for i in range(devices)])  12.6 us
    pallas_call x3, Pallas kernels, layer_step(): pl.pallas_call(kernel, out_shape=(jax.ShapeDtypeStruct((whole, width), jn...  12.4 us
  transfers between devices with their start and end apart: 19, of which 14 were waited for; matrix products, arithmetic and copies ran while one was open for 4% of the time, Pallas kernels for 21%

profile of v1, /device:TPU:1, one launch (start us, length us, event | category | flops | bytes accessed | tf_op | source)
XLA Modules:
  0.0 262.3 jit_solution(15270738314116137265)
XLA Ops:
  0.6 1.9 slice_bitcast_fusion.4
  2.5 1.6 pad_maximum_fusion
  4.1 5.0 %all-to-all-start = ((bf16[4,2048,128]{2,1,0:T(8,128)(2,1)}), bf16[4,2048,128]{2,1,0:T(8,128)(2,1)}, u32[]{:S(2)}, u32[]{:S(2)}) async-start(bf16[4,2048,128]{2,1,0:T(8,128)(2,1)} %pad_maximum_fusion), calls=%async_computation | async-start | bytes 4194304 | tf_op jit(solution)/shard_map/all_to_all | solution.py:343
  9.1 1.9 fusion
  11.9 2.1 gather_fusion
  14.0 2.9 %copy-done.11 = bf16[3,64,128,128]{3,2,1,0:T(8,128)(2,1)S(1)} copy-done((bf16[3,64,128,128]{3,2,1,0:T(8,128)(2,1)S(1)}, bf16[3,64,128,128]{3,2,1,0:T(8,128)(2,1)}, u32[]{:S(2)}) %copy-start.11) | copy-done | bytes 6291480
  16.9 10.3 %dense_adjacency.1.adj_ref = bf16[3,2048,2048]{2,1,0:T(8,128)(2,1)} custom-call(s32[3,64]{1,0:T(4,128)S(1)} %copy-done.15, s32[3,64]{1,0:T(4,128)S(1)} %copy-done.16, s32[3]{0:T(128)S(1)} %bitcast.88, bf16[3,64,128,128]{3,2,1,0:T(8,128)(2,1)S(1)} %copy-done.11), custom_call_target="tpu_custom_call" | custom-call | bytes 31457280 | tf_op jit(solution)/shard_map/dense_adjacency/pallas_call | solution.py:48
  27.4 18.7 %replaced_columns.1.cols_ref = bf16[3,2048,384]{2,1,0:T(8,128)(2,1)S(1)} custom-call(bf16[3,2048,2048]{2,1,0:T(8,128)(2,1)} %dense_adjacency.1.adj_ref, bf16[2048,384]{1,0:T(8,128)(2,1)S(1)} %copy-done.12), custom_call_target="tpu_custom_call" | custom-call | flops 9663676416 | bytes 29884416 | tf_op jit(solution)/shard_map/replaced_columns/pallas_call | solution.py:108
  46.1 2.2 copy-done.4
  50.4 8.1 %copy-done.2 = bf16[3,2048,2048]{2,1,0:T(8,128)(2,1)S(1)} copy-done((bf16[3,2048,2048]{2,1,0:T(8,128)(2,1)S(1)}, bf16[3,2048,2048]{2,1,0:T(8,128)(2,1)}, u32[]{:S(2)}) %copy-start.2) | copy-done | bytes 25165848
  58.5 9.5 %first_partial.1 = bf16[16,3,128,128]{3,2,1,0:T(8,128)(2,1)S(1)} custom-call(bf16[3,2048,2048]{2,1,0:T(8,128)(2,1)S(1)} %copy-done.2, bf16[2048,128]{1,0:T(8,128)(2,1)S(1)} %slice_bitcast_fusion.hist_ref, bf16[2048,128]{1,0:T(8,128)(2,1)S(1)} %constant_dynamic-slice_fusion.3.feat_ref, bf16[3,2048,128]{2,1,0:T(8,128)(2,1)S(1)} %broadcast_in_dim.20.mask_ref), custom_call_target="tpu_custom_call" | custom-call | flops 3221225472 | bytes 26738688 | tf_op jit(solution)/shard_map/first_partial/pallas_call | solution.py:78
  68.0 1.1 copy-done.10
  69.2 7.7 %all-to-all-start.1 = ((bf16[16,3,128,128]{3,2,1,0:T(8,128)(2,1)}), bf16[16,3,128,128]{3,2,1,0:T(8,128)(2,1)}, u32[]{:S(2)}, u32[]{:S(2)}) async-start(bf16[16,3,128,128]{3,2,1,0:T(8,128)(2,1)} %copy-done.10), calls=%async_computation.1 | async-start | bytes 3145728 | tf_op jit(solution)/shard_map/all_to_all | solution.py:382
  78.1 2.6 collective-permute-start.5
  81.9 21.2 %static_parts.1.static_ref = f32[3,3,2048,128]{3,2,1,0:T(8,128)S(1)} custom-call(bf16[3,2048,2048]{2,1,0:T(8,128)(2,1)} %dense_adjacency.1.adj_ref, bf16[4,2048,128]{2,1,0:T(8,128)(2,1)} %all-to-all-done.hist_ref, bf16[3,2048,128]{2,1,0:T(8,128)(2,1)S(1)} %broadcast_in_dim.20.mask_ref), custom_call_target="tpu_custom_call" | custom-call | flops 9663676416 | bytes 34603008 | tf_op jit(solution)/shard_map/static_parts/pallas_call | solution.py:141
  103.1 3.7 %copy-done.3 = f32[3,3,2048,128]{3,2,1,0:T(8,128)} copy-done((f32[3,3,2048,128]{3,2,1,0:T(8,128)}, f32[3,3,2048,128]{3,2,1,0:T(8,128)S(1)}, u32[]{:S(2)}) %copy-start.3) | copy-done | bytes 9437208
  106.8 1.7 convert_reduce_fusion.3
  108.6 2.1 collective-permute-start.2
  110.7 1.2 collective-permute-start.1
  111.9 1.2 pad_maximum_fusion.1.w_ref
  113.3 2.4 collective-permute-done.1
  116.8 5.8 %all-gather = bf16[8,384,128]{2,1,0:T(8,128)(2,1)S(1)} all-gather(bf16[4,384,128]{2,1,0:T(8,128)(2,1)S(1)} %pad_maximum_fusion.2), channel_id=2, replica_groups=mesh['section'=4,'vertex'=16,'feat'=2] {'feat'}, dimensions={0}, use_global_device_ids=true | all-gather | bytes 1179648 | tf_op jit(solution)/shard_map/all_gather | solution.py:392
  122.6 2.3 copy-done.5
  125.0 4.1 %layer_step.3 = (bf16[384,128]{1,0:T(8,128)(2,1)}, bf16[16,3,128,128]{3,2,1,0:T(8,128)(2,1)S(1)}) custom-call(s32[2]{0:T(128)S(1)} %pad_add_fusion.place_ref, bf16[2,4,384,128]{3,2,1,0:T(8,128)(2,1)S(1)} %bitcast.77, bf16[384,128]{1,0:T(8,128)(2,1)S(1)} %fusion.5.sup_ref, bf16[4,1024,128]{2,1,0:T(8,128)(2,1)S(1)} %pad_maximum_fusion.1.w_ref, ...), custom_call_target="tpu_custom_call" | custom-call | flops 704643072 | bytes 9437184 | tf_op jit(solution)/shard_map/layer_step/pallas_call | solution.py:214
  129.1 28.7 %all_to_all.25 = bf16[16,3,128,128]{3,2,1,0:T(8,128)(2,1)S(1)} all-to-all(bf16[16,3,128,128]{3,2,1,0:T(8,128)(2,1)S(1)} %get-tuple-element.11), channel_id=1, replica_groups=mesh['section'=4,'vertex'=16,'feat'=2] {'vertex'}, dimensions={0} | all-to-all | bytes 3145728 | tf_op jit(solution)/shard_map/all_to_all | solution.py:382
  158.3 1.2 collective-permute-start.7
  160.1 1.5 collective-permute-done.8
  161.6 1.6 collective-permute-done.7
  164.4 5.7 %all-gather.1 = bf16[8,384,128]{2,1,0:T(8,128)(2,1)S(1)} all-gather(bf16[4,384,128]{2,1,0:T(8,128)(2,1)S(1)} %pad_maximum_fusion.3), channel_id=3, replica_groups=mesh['section'=4,'vertex'=16,'feat'=2] {'feat'}, dimensions={0}, use_global_device_ids=true | all-gather | bytes 1179648 | tf_op jit(solution)/shard_map/all_gather | solution.py:392
  170.0 4.1 %layer_step.4 = (bf16[384,128]{1,0:T(8,128)(2,1)}, bf16[16,3,128,128]{3,2,1,0:T(8,128)(2,1)S(1)}) custom-call(s32[2]{0:T(128)S(1)} %pad_add_fusion.place_ref, bf16[2,4,384,128]{3,2,1,0:T(8,128)(2,1)S(1)} %bitcast.79, bf16[384,128]{1,0:T(8,128)(2,1)S(1)} %fusion.4.sup_ref, bf16[4,1024,128]{2,1,0:T(8,128)(2,1)S(1)} %pad_maximum_fusion.1.w_ref, ...), custom_call_target="tpu_custom_call" | custom-call | flops 704643072 | bytes 9437184 | tf_op jit(solution)/shard_map/layer_step/pallas_call | solution.py:214
  174.2 24.7 %all_to_all.26 = bf16[16,3,128,128]{3,2,1,0:T(8,128)(2,1)S(1)} all-to-all(bf16[16,3,128,128]{3,2,1,0:T(8,128)(2,1)S(1)} %get-tuple-element.12), channel_id=1, replica_groups=mesh['section'=4,'vertex'=16,'feat'=2] {'vertex'}, dimensions={0} | all-to-all | bytes 3145728 | tf_op jit(solution)/shard_map/all_to_all | solution.py:382
  201.0 1.8 collective-permute-done.11
  202.8 2.4 collective-permute-done.10
  206.2 5.2 %all-gather.2 = bf16[8,384,128]{2,1,0:T(8,128)(2,1)S(1)} all-gather(bf16[4,384,128]{2,1,0:T(8,128)(2,1)S(1)} %pad_maximum_fusion.4), channel_id=4, replica_groups=mesh['section'=4,'vertex'=16,'feat'=2] {'feat'}, dimensions={0}, use_global_device_ids=true | all-gather | bytes 1179648 | tf_op jit(solution)/shard_map/all_gather | solution.py:392
  211.4 4.1 %layer_step.5 = (bf16[384,128]{1,0:T(8,128)(2,1)}, bf16[16,3,128,128]{3,2,1,0:T(8,128)(2,1)S(1)}) custom-call(s32[2]{0:T(128)S(1)} %pad_add_fusion.place_ref, bf16[2,4,384,128]{3,2,1,0:T(8,128)(2,1)S(1)} %bitcast.81, bf16[384,128]{1,0:T(8,128)(2,1)S(1)} %fusion.3.sup_ref, bf16[4,1024,128]{2,1,0:T(8,128)(2,1)S(1)} %pad_maximum_fusion.1.w_ref, ...), custom_call_target="tpu_custom_call" | custom-call | flops 704643072 | bytes 9437184 | tf_op jit(solution)/shard_map/layer_step/pallas_call | solution.py:214
  215.6 1.1 copy-done.13
  216.7 4.5 %all-to-all-start.4 = ((bf16[16,3,128,128]{3,2,1,0:T(8,128)(2,1)}), bf16[16,3,128,128]{3,2,1,0:T(8,128)(2,1)}, u32[]{:S(2)}, u32[]{:S(2)}) async-start(bf16[16,3,128,128]{3,2,1,0:T(8,128)(2,1)} %copy-done.13), calls=%async_computation.4 | async-start | bytes 3145728 | tf_op jit(solution)/shard_map/all_to_all | solution.py:382
  221.3 1.2 whole_rows.4.refs_0_
  223.8 11.6 %collective-permute-done.12 = bf16[384,512]{1,0:T(8,128)(2,1)} collective-permute-done((bf16[384,512]{1,0:T(8,128)(2,1)S(1)}, bf16[384,512]{1,0:T(8,128)(2,1)}, u32[]{:S(2)}, u32[]{:S(2)}) %collective-permute-start.12) | collective-permute-done | bytes 393248 | tf_op jit(solution)/shard_map/ppermute | solution.py:19
  235.4 1.1 broadcast_select_fusion.1.fresh_ref
  236.5 2.9 %replace_rows.1 = bf16[2048,512]{1,0:T(8,128)(2,1)} custom-call(bf16[2048,512]{1,0:T(8,128)(2,1)S(1)} %bitcast.76, s32[1,384]{1,0:T(1,128)S(1)} %bitcast.87, bf16[384,512]{1,0:T(8,128)(2,1)S(1)} %broadcast_select_fusion.1.fresh_ref), custom_call_target="tpu_custom_call" | custom-call | flops 805306368 | bytes 4194304 | tf_op jit(solution)/shard_map/replace_rows/pallas_call | solution.py:311
  239.4 7.0 %all-to-all-done.4 = bf16[16,3,128,128]{3,2,1,0:T(8,128)(2,1)} async-done(((bf16[16,3,128,128]{3,2,1,0:T(8,128)(2,1)}), bf16[16,3,128,128]{3,2,1,0:T(8,128)(2,1)}, u32[]{:S(2)}, u32[]{:S(2)}) %all-to-all-start.4) | async-done | bytes 1572896 | tf_op jit(solution)/shard_map/all_to_all | solution.py:382
  246.4 1.7 convert_reduce_fusion
  250.7 1.9 collective-permute-done.15
  252.6 2.3 collective-permute-done.14
  254.9 1.5 collective-permute-done.13
  256.4 4.5 %all-gather.3 = bf16[8,384,128]{2,1,0:T(8,128)(2,1)S(1)} all-gather(bf16[4,384,128]{2,1,0:T(8,128)(2,1)S(1)} %pad_maximum_fusion.5), channel_id=5, replica_groups=mesh['section'=4,'vertex'=16,'feat'=2] {'feat'}, dimensions={0}, use_global_device_ids=true | all-gather | bytes 1179648 | tf_op jit(solution)/shard_map/all_gather | solution.py:392
  261.0 1.3 whole_rows.7
  (90 shorter events, 15.9 us)
Async XLA Ops:
  0.6 11.3 %copy-start = (bf16[2048,512]{1,0:T(8,128)(2,1)S(1)}, bf16[2048,512]{1,0:T(8,128)(2,1)}, u32[]{:S(2)}) copy-start(bf16[2048,512]{1,0:T(8,128)(2,1)} %param.9) | copy-start | bytes 6291460
  4.1 5.0 %copy-start.20 = (s32[3,128]{1,0:T(4,128)S(1)}, s32[3,128]{1,0:T(4,128)}, u32[]{:S(2)}) copy-start(s32[3,128]{1,0:T(4,128)} %param.16) | copy-start | bytes 4612
  4.1 44.2 %all-to-all-start = ((bf16[4,2048,128]{2,1,0:T(8,128)(2,1)}), bf16[4,2048,128]{2,1,0:T(8,128)(2,1)}, u32[]{:S(2)}, u32[]{:S(2)}) async-start(bf16[4,2048,128]{2,1,0:T(8,128)(2,1)} %pad_maximum_fusion), calls=%async_computation | async-start | bytes 4194304 | tf_op jit(solution)/shard_map/all_to_all | solution.py:343
  11.3 2.7 %copy-start.15 = (s32[3,64]{1,0:T(4,128)S(1)}, s32[3,64]{1,0:T(4,128)}, u32[]{:S(2)}) copy-start(s32[3,64]{1,0:T(4,128)} %rows_ref.1) | copy-start | bytes 2308
  11.3 2.7 %copy-start.16 = (s32[3,64]{1,0:T(4,128)S(1)}, s32[3,64]{1,0:T(4,128)}, u32[]{:S(2)}) copy-start(s32[3,64]{1,0:T(4,128)} %cols_ref.1) | copy-start | bytes 2308
  11.4 2.7 %copy-start.17 = (s32[3,1]{0,1:T(1,128)S(1)}, s32[3,1]{0,1:T(1,128)}, u32[]{:S(2)}) copy-start(s32[3,1]{0,1:T(1,128)} %param.15) | copy-start | bytes 40
  14.0 63.0 %copy-start.18 = (bf16[384,512]{1,0:T(8,128)(2,1)}, bf16[384,512]{1,0:T(8,128)(2,1)S(1)}, u32[]{:S(2)}) copy-start(bf16[384,512]{1,0:T(8,128)(2,1)S(1)} %gather_fusion) | copy-start | bytes 1179652
  14.0 2.9 %copy-start.11 = (bf16[3,64,128,128]{3,2,1,0:T(8,128)(2,1)S(1)}, bf16[3,64,128,128]{3,2,1,0:T(8,128)(2,1)}, u32[]{:S(2)}) copy-start(bf16[3,64,128,128]{3,2,1,0:T(8,128)(2,1)} %values_ref.1) | copy-start | bytes 18874372
  16.9 10.5 %copy-start.12 = (bf16[2048,384]{1,0:T(8,128)(2,1)S(1)}, bf16[2048,384]{1,0:T(8,128)(2,1)}, u32[]{:S(2)}) copy-start(bf16[2048,384]{1,0:T(8,128)(2,1)} %get-tuple-element.24.sel_ref) | copy-start | bytes 4718596
  46.1 2.2 copy-start.4
  50.4 8.2 %copy-start.2 = (bf16[3,2048,2048]{2,1,0:T(8,128)(2,1)S(1)}, bf16[3,2048,2048]{2,1,0:T(8,128)(2,1)}, u32[]{:S(2)}) copy-start(bf16[3,2048,2048]{2,1,0:T(8,128)(2,1)} %dense_adjacency.1.adj_ref) | copy-start | bytes 75497472
  68.0 1.1 copy-start.10
  69.2 7.9 %copy-start.6 = (bf16[1,1024,512]{2,1,0:T(8,128)(2,1)S(1)}, bf16[1,1024,512]{2,1,0:T(8,128)(2,1)}, u32[]{:S(2)}) copy-start(bf16[1,1024,512]{2,1,0:T(8,128)(2,1)} %param.11) | copy-start | bytes 3145732
  69.2 37.7 %all-to-all-start.1 = ((bf16[16,3,128,128]{3,2,1,0:T(8,128)(2,1)}), bf16[16,3,128,128]{3,2,1,0:T(8,128)(2,1)}, u32[]{:S(2)}, u32[]{:S(2)}) async-start(bf16[16,3,128,128]{3,2,1,0:T(8,128)(2,1)} %copy-done.10), calls=%async_computation.1 | async-start | bytes 3145728 | tf_op jit(solution)/shard_map/all_to_all | solution.py:382
  76.9 26.2 %copy-start.21 = (pred[384]{0:T(512)(128)(4,1)}, pred[384]{0:T(512)(128)(4,1)S(1)}, u32[]{:S(2)}) copy-start(pred[384]{0:T(512)(128)(4,1)S(1)} %compare_and_fusion) | copy-start | bytes 1156
  77.1 122.1 %copy-start.19 = (bf16[384,512]{1,0:T(8,128)(2,1)}, bf16[384,512]{1,0:T(8,128)(2,1)S(1)}, u32[]{:S(2)}) copy-start(bf16[384,512]{1,0:T(8,128)(2,1)S(1)} %broadcast_select_fusion) | copy-start | bytes 1179652
  78.1 33.8 %collective-permute-start.5 = (bf16[1024,128]{1,0:T(8,128)(2,1)}, bf16[1024,128]{1,0:T(8,128)(2,1)}, u32[]{:S(2)}, u32[]{:S(2)}) collective-permute-start(bf16[1024,128]{1,0:T(8,128)(2,1)} %get-tuple-element.21), channel_id=1, source_target_pairs={{0,96},{32,0},{64,32},{96,64},{1,97},{33,1},{65,33},{97,65},{2,98}... | collective-permute-start | bytes 786440 | tf_op jit(solution)/shard_map/ppermute | solution.py:19
  80.7 31.2 %collective-permute-start.4 = (bf16[1024,128]{1,0:T(8,128)(2,1)}, bf16[1024,128]{1,0:T(8,128)(2,1)}, u32[]{:S(2)}, u32[]{:S(2)}) collective-permute-start(bf16[1024,128]{1,0:T(8,128)(2,1)} %get-tuple-element.22), channel_id=1, source_target_pairs={{0,64},{32,96},{64,0},{96,32},{1,65},{33,97},{65,1},{97,33},{2,66}... | collective-permute-start | bytes 786440 | tf_op jit(solution)/shard_map/ppermute | solution.py:19
  81.3 30.6 %collective-permute-start.3 = (bf16[1024,128]{1,0:T(8,128)(2,1)}, bf16[1024,128]{1,0:T(8,128)(2,1)}, u32[]{:S(2)}, u32[]{:S(2)}) collective-permute-start(bf16[1024,128]{1,0:T(8,128)(2,1)} %get-tuple-element.23), channel_id=1, source_target_pairs={{0,32},{32,64},{64,96},{96,0},{1,33},{33,65},{65,97},{97,1},{2,34}... | collective-permute-start | bytes 786440 | tf_op jit(solution)/shard_map/ppermute | solution.py:19
  103.1 3.7 %copy-start.3 = (f32[3,3,2048,128]{3,2,1,0:T(8,128)}, f32[3,3,2048,128]{3,2,1,0:T(8,128)S(1)}, u32[]{:S(2)}) copy-start(f32[3,3,2048,128]{3,2,1,0:T(8,128)S(1)} %static_parts.1.static_ref) | copy-start | bytes 28311556
  108.6 4.8 %collective-permute-start.2 = (bf16[384,128]{1,0:T(8,128)(2,1)S(1)}, bf16[384,128]{1,0:T(8,128)(2,1)S(1)}, u32[]{:S(2)}, u32[]{:S(2)}) collective-permute-start(bf16[384,128]{1,0:T(8,128)(2,1)S(1)} %fusion.5.sup_ref), channel_id=1, source_target_pairs={{0,96},{32,0},{64,32},{96,64},{1,97},{33,1},{65,33},{97,65},{2,98}... | collective-permute-start | bytes 294920 | tf_op jit(solution)/shard_map/ppermute | solution.py:19
  110.7 5.0 %collective-permute-start.1 = (bf16[384,128]{1,0:T(8,128)(2,1)S(1)}, bf16[384,128]{1,0:T(8,128)(2,1)S(1)}, u32[]{:S(2)}, u32[]{:S(2)}) collective-permute-start(bf16[384,128]{1,0:T(8,128)(2,1)S(1)} %fusion.5.sup_ref), channel_id=1, source_target_pairs={{0,64},{32,96},{64,0},{96,32},{1,65},{33,97},{65,1},{97,33},{2,66}... | collective-permute-start | bytes 294920 | tf_op jit(solution)/shard_map/ppermute | solution.py:19
  111.9 4.8 %collective-permute-start = (bf16[384,128]{1,0:T(8,128)(2,1)S(1)}, bf16[384,128]{1,0:T(8,128)(2,1)S(1)}, u32[]{:S(2)}, u32[]{:S(2)}) collective-permute-start(bf16[384,128]{1,0:T(8,128)(2,1)S(1)} %fusion.5.sup_ref), channel_id=1, source_target_pairs={{0,32},{32,64},{64,96},{96,0},{1,33},{33,65},{65,97},{97,1},{2,34}... | collective-permute-start | bytes 294920 | tf_op jit(solution)/shard_map/ppermute | solution.py:19
  122.6 2.3 copy-start.5
  158.1 3.5 %collective-permute-start.8 = (bf16[384,128]{1,0:T(8,128)(2,1)S(1)}, bf16[384,128]{1,0:T(8,128)(2,1)S(1)}, u32[]{:S(2)}, u32[]{:S(2)}) collective-permute-start(bf16[384,128]{1,0:T(8,128)(2,1)S(1)} %fusion.4.sup_ref), channel_id=1, source_target_pairs={{0,96},{32,0},{64,32},{96,64},{1,97},{33,1},{65,33},{97,65},{2,98}... | collective-permute-start | bytes 294920 | tf_op jit(solution)/shard_map/ppermute | solution.py:19
  158.3 5.0 %collective-permute-start.7 = (bf16[384,128]{1,0:T(8,128)(2,1)S(1)}, bf16[384,128]{1,0:T(8,128)(2,1)S(1)}, u32[]{:S(2)}, u32[]{:S(2)}) collective-permute-start(bf16[384,128]{1,0:T(8,128)(2,1)S(1)} %fusion.4.sup_ref), channel_id=1, source_target_pairs={{0,64},{32,96},{64,0},{96,32},{1,65},{33,97},{65,1},{97,33},{2,66}... | collective-permute-start | bytes 294920 | tf_op jit(solution)/shard_map/ppermute | solution.py:19
  159.5 4.8 %collective-permute-start.6 = (bf16[384,128]{1,0:T(8,128)(2,1)S(1)}, bf16[384,128]{1,0:T(8,128)(2,1)S(1)}, u32[]{:S(2)}, u32[]{:S(2)}) collective-permute-start(bf16[384,128]{1,0:T(8,128)(2,1)S(1)} %fusion.4.sup_ref), channel_id=1, source_target_pairs={{0,32},{32,64},{64,96},{96,0},{1,33},{33,65},{65,97},{97,1},{2,34}... | collective-permute-start | bytes 294920 | tf_op jit(solution)/shard_map/ppermute | solution.py:19
  199.2 3.5 %collective-permute-start.11 = (bf16[384,128]{1,0:T(8,128)(2,1)S(1)}, bf16[384,128]{1,0:T(8,128)(2,1)S(1)}, u32[]{:S(2)}, u32[]{:S(2)}) collective-permute-start(bf16[384,128]{1,0:T(8,128)(2,1)S(1)} %fusion.3.sup_ref), channel_id=1, source_target_pairs={{0,96},{32,0},{64,32},{96,64},{1,97},{33,1},{65,33},{97,65},{2,98}... | collective-permute-start | bytes 294920 | tf_op jit(solution)/shard_map/ppermute | solution.py:19
  200.2 5.0 %collective-permute-start.10 = (bf16[384,128]{1,0:T(8,128)(2,1)S(1)}, bf16[384,128]{1,0:T(8,128)(2,1)S(1)}, u32[]{:S(2)}, u32[]{:S(2)}) collective-permute-start(bf16[384,128]{1,0:T(8,128)(2,1)S(1)} %fusion.3.sup_ref), channel_id=1, source_target_pairs={{0,64},{32,96},{64,0},{96,32},{1,65},{33,97},{65,1},{97,33},{2,66}... | collective-permute-start | bytes 294920 | tf_op jit(solution)/shard_map/ppermute | solution.py:19
  200.8 5.4 %collective-permute-start.9 = (bf16[384,128]{1,0:T(8,128)(2,1)S(1)}, bf16[384,128]{1,0:T(8,128)(2,1)S(1)}, u32[]{:S(2)}, u32[]{:S(2)}) collective-permute-start(bf16[384,128]{1,0:T(8,128)(2,1)S(1)} %fusion.3.sup_ref), channel_id=1, source_target_pairs={{0,32},{32,64},{64,96},{96,0},{1,33},{33,65},{65,97},{97,1},{2,34}... | collective-permute-start | bytes 294920 | tf_op jit(solution)/shard_map/ppermute | solution.py:19
  211.4 4.1 %copy-start.8 = (bf16[8,384,128]{2,1,0:T(8,128)(2,1)}, bf16[8,384,128]{2,1,0:T(8,128)(2,1)S(1)}, u32[]{:S(2)}) copy-start(bf16[8,384,128]{2,1,0:T(8,128)(2,1)S(1)} %all-gather.2) | copy-start | bytes 2359300
  215.6 1.1 copy-start.13
  216.7 4.5 %copy-start.14 = (f32[4]{0:T(128)S(1)}, f32[4]{0:T(128)}, u32[]{:S(2)}) copy-start(f32[4]{0:T(128)} %constant.70.clone.betas_ref) | copy-start | bytes 52
  216.7 29.7 %all-to-all-start.4 = ((bf16[16,3,128,128]{3,2,1,0:T(8,128)(2,1)}), bf16[16,3,128,128]{3,2,1,0:T(8,128)(2,1)}, u32[]{:S(2)}, u32[]{:S(2)}) async-start(bf16[16,3,128,128]{3,2,1,0:T(8,128)(2,1)} %copy-done.13), calls=%async_computation.4 | async-start | bytes 3145728 | tf_op jit(solution)/shard_map/all_to_all | solution.py:382
  221.3 1.8 copy-start.9
  223.1 13.4 %copy-start.7 = (bf16[1,2048,512]{2,1,0:T(8,128)(2,1)S(1)}, bf16[1,2048,512]{2,1,0:T(8,128)(2,1)}, u32[]{:S(2)}) copy-start(bf16[1,2048,512]{2,1,0:T(8,128)(2,1)} %param.10) | copy-start | bytes 6291460
  223.7 11.7 %collective-permute-start.12 = (bf16[384,512]{1,0:T(8,128)(2,1)S(1)}, bf16[384,512]{1,0:T(8,128)(2,1)}, u32[]{:S(2)}, u32[]{:S(2)}) collective-permute-start(bf16[384,512]{1,0:T(8,128)(2,1)S(1)} %whole_rows.6.refs_0_), channel_id=1, source_target_pairs={{0,32},{32,64},{64,96},{96,0},{1,33},{33,65},{65,97},{97,1},{2,34}... | collective-permute-start | bytes 1179656 | tf_op jit(solution)/shard_map/ppermute | solution.py:19
  249.1 3.5 %collective-permute-start.15 = (bf16[384,128]{1,0:T(8,128)(2,1)S(1)}, bf16[384,128]{1,0:T(8,128)(2,1)S(1)}, u32[]{:S(2)}, u32[]{:S(2)}) collective-permute-start(bf16[384,128]{1,0:T(8,128)(2,1)S(1)} %fusion.2), channel_id=1, source_target_pairs={{0,96},{32,0},{64,32},{96,64},{1,97},{33,1},{65,33},{97,65},{2,98}... | collective-permute-start | bytes 294920 | tf_op jit(solution)/shard_map/ppermute | solution.py:19
  249.8 5.0 %collective-permute-start.14 = (bf16[384,128]{1,0:T(8,128)(2,1)S(1)}, bf16[384,128]{1,0:T(8,128)(2,1)S(1)}, u32[]{:S(2)}, u32[]{:S(2)}) collective-permute-start(bf16[384,128]{1,0:T(8,128)(2,1)S(1)} %fusion.2), channel_id=1, source_target_pairs={{0,64},{32,96},{64,0},{96,32},{1,65},{33,97},{65,1},{97,33},{2,66}... | collective-permute-start | bytes 294920 | tf_op jit(solution)/shard_map/ppermute | solution.py:19
  250.5 5.9 %collective-permute-start.13 = (bf16[384,128]{1,0:T(8,128)(2,1)S(1)}, bf16[384,128]{1,0:T(8,128)(2,1)S(1)}, u32[]{:S(2)}, u32[]{:S(2)}) collective-permute-start(bf16[384,128]{1,0:T(8,128)(2,1)S(1)} %fusion.2), channel_id=1, source_target_pairs={{0,32},{32,64},{64,96},{96,0},{1,33},{33,65},{65,97},{97,1},{2,34}... | collective-permute-start | bytes 294920 | tf_op jit(solution)/shard_map/ppermute | solution.py:19
  256.4 5.9 %copy-start.1 = (bf16[2048,512]{1,0:T(8,128)(2,1)S(1)}, bf16[2048,512]{1,0:T(8,128)(2,1)}, u32[]{:S(2)}) copy-start(bf16[2048,512]{1,0:T(8,128)(2,1)} %param.9) | copy-start | bytes 6291460
